TPU v7x, 32 devices: a whole 2x2x4 slice. The times are simulated.
32 devices in a mesh: group: 2 (over y), ctx: 4 (over z), head: 4 (over x, core).
Axes of the slice: x: 2, y: 2, z: 4, core: 2. Of those that a mesh axis runs over, the one named last changes fastest.
Arguments:
- head_input: bfloat16 [4096, 8192], P(('group', 'ctx'), 'head'), parts along dimension 0, may hold values from -6 to 6
- gate_input: bfloat16 [4096, 8192], P(('group', 'ctx'), 'head'), parts along dimension 0, may hold values from -40 to 40
- input_map: bfloat16 [4096, 2048], P(('group', 'ctx'), 'head'), parts along dimension 0, may hold values from -4 to 4
- output_map: bfloat16 [4096, 2048], P(('group', 'ctx'), 'head'), parts along dimension 0, may hold values from -4 to 4
- step_size: float32 [128, 4096], P('head', ('group', 'ctx')), parts along dimension 1, may hold values from 0.1 to 0.4
- decays: float32 [128, 4096], P('head', ('group', 'ctx')), parts along dimension 1, may hold values from 0.45 to 1
- bypass_scale: float32 [128], P('head'), may hold values from 1 to 4
- norm_gain: bfloat16 [8192], P('head'), may hold values from 0.099609375 to 1.8984375
- out_weight: bfloat16 [8192, 4096], P('head', 'ctx'), may hold values from -0.0625 to 0.0625
Outputs:
- layer_out: bfloat16 [4096, 4096], P(('group', 'ctx', 'head')), parts along dimension 0
There are 2 independent parts, one for each index of `group`. A program takes and returns all parts, laid end to end along the dimension named above; an argument that names none is the same for every part. Nothing has to cross between parts.
All inputs are finite; a program needn't handle non-finite values.
Results may differ from a plain program's by a relative error of at most 0.014.
Values may be sent and summed in bfloat16 or wider, within the bound.
A program may use at most 128 MiB of HBM per device.

v0:
```python
import jax
import jax.numpy as jnp
from jax import lax
from jax.sharding import PartitionSpec as P

HEADP = 64
STATE = 256
STRETCH = 128


def carried_in(shard, axis, combine, identity):
    size, position = (lax.axis_size(axis), lax.axis_index(axis))
    everything = jax.tree.map(
        lambda part, kind: lax.all_gather(part.astype(kind), axis),
        shard,
        (jnp.bfloat16, jnp.bfloat16),
    )
    start = jax.tree.map(
        lambda part, zero: jnp.broadcast_to(jnp.asarray(zero, part.dtype), part.shape),
        shard,
        identity,
    )

    def lap(k, before):
        reached = k < position
        new = combine(
            before, jax.tree.map(lambda part, own: part[k].astype(own.dtype), everything, shard)
        )
        return jax.tree.map(lambda a, b: jnp.where(reached, a, b), new, before)

    return lax.fori_loop(0, size, lap, start)


def block_term_values(inputs, in_maps, out_maps, steps, decays):
    count, length, groups, per_group, channels = inputs.shape
    ramps = jnp.cumsum(jnp.log(decays), axis=-1)
    rows = lax.broadcasted_iota(jnp.int32, (length, length), 0)
    cols = lax.broadcasted_iota(jnp.int32, (length, length), 1)
    lower = rows >= cols
    spread = ramps[:, :, :, None] - ramps[:, :, None, :]
    within_decay = jnp.where(lower, jnp.exp(jnp.where(lower, spread, 0.0)), 0.0)
    scores = jnp.einsum("kqgn,ksgn->kgqs", out_maps, in_maps, preferred_element_type=jnp.float32)
    mixing = within_decay.reshape(count, groups, per_group, length, length) * scores[:, :, None]
    mixing = mixing * steps.reshape(count, groups, per_group, 1, length)
    mixing = mixing.astype(jnp.bfloat16)
    within = jnp.einsum("kgjqs,ksgjp->kqgjp", mixing, inputs, preferred_element_type=jnp.float32)
    tails = jnp.exp(ramps[:, :, -1:] - ramps) * steps
    tails = jnp.transpose(tails.reshape(count, groups, per_group, length), (0, 3, 1, 2))[..., None]
    weighted = (inputs.astype(jnp.float32) * tails).astype(jnp.bfloat16)
    block_state = jnp.einsum(
        "ksgjp,ksgn->kgjpn", weighted, in_maps, preferred_element_type=jnp.float32
    )
    accumulated_sums_list = jnp.exp(ramps[:, :, -1]).reshape(count, groups, per_group)
    entry = jnp.transpose(jnp.exp(ramps).reshape(count, groups, per_group, length), (0, 3, 1, 2))[
        ..., None
    ]
    return (within, block_state, accumulated_sums_list, entry)


def join_states(earlier, later):
    early_decay, early_state = earlier
    late_decay, late_state = later
    return (early_decay * late_decay, late_decay[..., None, None] * early_state + late_state)


def shards(
    head_input,
    gate_input,
    input_map,
    output_map,
    step_size,
    decays,
    bypass_scale,
    norm_gain,
    out_weight,
):
    tok_rows, width = head_input.shape
    heads = step_size.shape[0]
    groups = input_map.shape[1] // STATE
    per_group = heads // groups
    blocks = tok_rows // STRETCH
    inputs = head_input.reshape(blocks, STRETCH, groups, per_group, HEADP)
    in_maps = input_map.reshape(blocks, STRETCH, groups, STATE)
    out_maps = output_map.reshape(blocks, STRETCH, groups, STATE)
    steps = jnp.transpose(step_size.reshape(heads, blocks, STRETCH), (1, 0, 2))
    rates = jnp.transpose(decays.reshape(heads, blocks, STRETCH), (1, 0, 2))
    within, block_state, accumulated_sums_list, entry = block_term_values(
        inputs, in_maps, out_maps, steps, rates
    )

    def advance(carry, item):
        state, lead = carry
        total, piece = item
        return ((total[..., None, None] * state + piece, total * lead), (state, lead))

    empty_state = jnp.zeros((groups, per_group, HEADP, STATE), jnp.float32)
    unit_decay = jnp.ones((groups, per_group), jnp.float32)
    (local_state, local_decay), (local_entering, leads) = lax.scan(
        advance, (empty_state, unit_decay), (accumulated_sums_list, block_state)
    )
    incoming_decay, incoming = carried_in(
        (local_decay, local_state), "ctx", join_states, (unit_decay, empty_state)
    )
    entering = local_entering + leads[..., None, None] * incoming
    carried = (
        jnp.einsum(
            "kqgn,kgjpn->kqgjp",
            out_maps.astype(jnp.float32),
            entering,
            precision=lax.Precision.HIGHEST,
        )
        * entry
    )
    skip = bypass_scale.reshape(groups, per_group, 1)
    mamba_out = (within + carried + skip * inputs.astype(jnp.float32)).reshape(tok_rows, width)
    gated = mamba_out * jax.nn.silu(gate_input.astype(jnp.float32))
    grouped = gated.reshape(tok_rows, groups, -1)
    factor = lax.rsqrt(jnp.mean(grouped * grouped, axis=-1, keepdims=True) + 1e-05)
    normed = ((grouped * factor).reshape(tok_rows, width) * norm_gain.astype(jnp.float32)).astype(
        jnp.bfloat16
    )
    terms = jnp.dot(
        normed,
        lax.all_gather(out_weight, "ctx", axis=1, tiled=True),
        preferred_element_type=jnp.float32,
    )
    summed = lax.psum_scatter(terms.astype(jnp.bfloat16), "head", scatter_dimension=0, tiled=True)
    return summed


def solution(mesh):
    return jax.shard_map(
        shards,
        mesh=mesh,
        in_specs=(
            P(("group", "ctx"), "head"),
            P(("group", "ctx"), "head"),
            P(("group", "ctx"), "head"),
            P(("group", "ctx"), "head"),
            P("head", ("group", "ctx")),
            P("head", ("group", "ctx")),
            P("head"),
            P("head"),
            P("head", "ctx"),
        ),
        out_specs=P(("group", "ctx", "head"), None),
        check_vma=False,
    )
```

profile of v0, /device:TPU:0, one launch (start us, length us, event | category | flops | bytes accessed | tf_op | source)
XLA Modules:
  0.0 478.2 jit_solution(10169969477722998015)
XLA Ops:
  8.8 7.1 %reshape.83 = bf16[4,128,2,16,64]{4,3,2,1,0:T(8,128)(2,1)} reshape(bf16[512,2048]{1,0:T(8,128)(2,1)} %param.13) | data formatting | bytes 4194304 | tf_op jit(solution)/shard_map/reshape | solution.py:82
  15.9 6.5 %copy.27 = bf16[4,128,2,16,64]{1,4,3,2,0:T(8,128)(2,1)} copy(bf16[4,128,2,16,64]{4,3,2,1,0:T(8,128)(2,1)} %reshape.83) | data formatting | bytes 4194304 | tf_op jit(solution)/shard_map/reshape | solution.py:82
  22.7 6.1 %fusion.23 = f32[4,2,16,64,256]{4,3,2,1,0:T(8,128)} fusion(bf16[4,128,2,16,64]{1,4,3,2,0:T(8,128)(2,1)} %copy.27, f32[4,128,2,16]{1,3,2,0:T(8,128)S(1)} %bitcast.92, bf16[4,128,2,256,1]{3,2,1,0,4:T(2,128)(2,1)S(1)} %bitcast.89), kind=kOutput, calls=%fused_computation.39 | convolution fusion | flops 540016640 | bytes 11075584 | tf_op jit(solution)/shard_map/ksgjp,ksgn->kgjpn/dot_general | solution.py:50
  28.8 14.3 %while.31 = (s32[]{:T(128)}, f32[2,16,64,256]{3,2,1,0:T(8,128)S(1)}, f32[2,16]{1,0:T(2,128)S(1)}, f32[4,2,16,64,256]{4,3,2,1,0:T(8,128)}, f32[4,2,16]{2,1,0:T(2,...) while((s32[]{:T(128)}, ...), condition=%wide.region_2.3_spmd.clone, body=%wide.region_1.2_spmd.clone.sunk | while | flops 2097251 | bytes 10489078 | solution.py:98
  28.8 1.5 bitcast_dynamic-update-slice_fusion.4
  30.3 2.0 bitcast_add_fusion.2
  33.9 2.0 bitcast_add_fusion.2
  37.5 2.0 bitcast_add_fusion.2
  41.0 2.0 bitcast_add_fusion.2
  46.3 3.9 copy.32
  50.3 12.9 %all-gather.2 = bf16[4,2,16]{2,1,0:T(2,128)(2,1)S(1)} all-gather(bf16[1,2,16]{2,1,0:T(2,128)(2,1)S(1)} %convert_bitcast_fusion), channel_id=2, replica_groups=mesh['group'=2,'ctx'=4,'head'=4] {'ctx'}, dimensions={0}, use_global_device_ids=true | all-gather | bytes 320 | tf_op jit(solution)/shard_map/all_gather | solution.py:14
  64.3 63.6 %all-gather.8.cloned.1.call-done = bf16[8,16,64,256]{3,2,1,0:T(8,128)(2,1)} async-done(((bf16[2,16,64,256]{3,2,1,0:T(8,128)(2,1)}), bf16[8,16,64,256]{3,2,1,0:T(8,128)(2,1)}) %all-gather.8.cloned.1.call-update) | async-done | bytes 4194320 | tf_op jit(solution)/shard_map/all_gather | solution.py:14
  127.9 9.2 %while.32 = (s32[]{:T(128)}, f32[2,16,64,256]{3,2,1,0:T(8,128)S(1)}, s32[]{:T(128)}, bf16[4,2,16]{2,1,0:T(2,128)(2,1)S(1)}, bf16[4,2,16,64,256]{4,3,2,1,0:T(8,128)(2,1)}, /*index=5*/s32[]{:T(128)}, s32[]{:T(128)}) while((s32[]{:T(128)}, f32[2,16,64,256]{3,2,1,0:T(8,128)S(1)}, s32[]{:T(128)}, bf16[4,2,16]{2,1,0:T(2,128)(2,1)S(1)}, ...), condition=%wide.region_4.5_spmd.clone, body=%wide.region_3.4_spmd.clone.sunk | while | flops 2621476 | bytes 5243305 | solution.py:31
  127.9 2.2 fusion.40
  130.1 2.2 fusion.40
  132.4 2.2 fusion.40
  134.7 2.4 fusion.40
  137.1 8.0 %fusion.2 = f32[4,2,16,64,128]{4,3,2,1,0:T(8,128)S(1)} fusion(f32[4,2,16,64,256]{4,3,2,1,0:T(8,128)} %get-tuple-element.139, f32[2,16,64,256]{3,2,1,0:T(8,128)S(1)} %get-tuple-element.143, f32[4,2,16]{2,1,0:T(2,128)S(1)} %get-tuple-element.140, bf16[4,128,2,256,1]{3,2,1,0,4:T(2,128)(2,1)S(1)} %bitcast.88), kind=kOutput, calls=%fused_computation.9 | convolution fusion | flops 3225419776 | bytes 15204864 | tf_op jit(solution)/shard_map/kqgn,kgjpn->kqgjp/dot_general | solution.py:106
  145.1 3.6 fusion.7
  148.8 3.6 copy.31
  153.8 1.7 fusion.13
  155.5 259.2 %all-gather.6.cloned.1.call-done = bf16[2048,4096]{1,0:T(8,128)(2,1)} async-done(((bf16[2048,1024]{1,0:T(8,128)(2,1)}), bf16[2048,4096]{1,0:T(8,128)(2,1)}) %all-gather.6.cloned.1.call-update) | async-done | bytes 16777232 | tf_op jit(solution)/shard_map/all_gather | solution.py:124
  414.8 14.0 %convolution_convert_fusion = bf16[512,4096]{1,0:T(8,128)(2,1)} fusion(bf16[512,2048]{0,1:T(8,128)(2,1)S(1)} %fusion.13, bf16[2048,4096]{1,0:T(8,128)(2,1)} %all-gather.6.cloned.1.call-done), kind=kOutput, calls=%fused_computation.13 | convolution fusion | flops 8592031744 | bytes 23068672 | tf_op jit(solution)/shard_map/dot_general | solution.py:122
  428.8 42.8 %reduce-scatter.2.cloned.1.call-done = bf16[128,4096]{1,0:T(8,128)(2,1)} async-done(((bf16[512,4096]{1,0:T(8,128)(2,1)}), bf16[128,4096]{1,0:T(8,128)(2,1)}) %reduce-scatter.2.cloned.1.call-update) | async-done | bytes 1048592 | tf_op jit(solution)/shard_map/reduce_scatter | solution.py:127
  (59 shorter events, 12.9 us)
Async XLA Ops:
  6.5 16.1 %copy-start = (f32[32,512]{1,0:T(8,128)S(1)}, f32[32,512]{1,0:T(8,128)}, u32[]{:S(2)}) copy-start(f32[32,512]{1,0:T(8,128)} %param.17) | copy-start | bytes 196612
  6.5 121.3 %all-gather.8.cloned.1.call-start = ((), (), s32[]{:S(2)}) async-start(), calls=%async_computation.3 | async-start | bytes 5242880 | tf_op jit(solution)/shard_map/all_gather | solution.py:14
  15.9 6.5 %copy-start.5 = (bf16[512,512]{1,0:T(8,128)(2,1)S(1)}, bf16[512,512]{1,0:T(8,128)(2,1)}, u32[]{:S(2)}) copy-start(bf16[512,512]{1,0:T(8,128)(2,1)} %param.15) | copy-start | bytes 1572868
  43.1 3.2 copy-start.7
  44.2 6.0 %copy-start.6 = (bf16[2048]{0:T(1024)(128)(2,1)S(1)}, bf16[2048]{0:T(1024)(128)(2,1)}, u32[]{:S(2)}) copy-start(bf16[2048]{0:T(1024)(128)(2,1)} %param.20) | copy-start | bytes 12292
  44.2 370.5 %all-gather.6.cloned.1.call-start = ((), (), s32[]{:S(2)}) async-start(), calls=%async_computation.1 | async-start | bytes 20971520 | tf_op jit(solution)/shard_map/all_gather | solution.py:124
  45.0 426.6 %reduce-scatter.2.cloned.1.call-start = ((), (), s32[]{:S(2)}) async-start(), calls=%async_computation.2 | async-start | bytes 5242880 | tf_op jit(solution)/shard_map/reduce_scatter | solution.py:127
  137.1 8.0 %copy-start.3 = (bf16[4,128,2,16,64]{1,4,3,2,0:T(8,128)(2,1)S(1)}, bf16[4,128,2,16,64]{1,4,3,2,0:T(8,128)(2,1)}, u32[]{:S(2)}) copy-start(bf16[4,128,2,16,64]{1,4,3,2,0:T(8,128)(2,1)} %copy.27) | copy-start | bytes 6291460
  137.1 8.0 %copy-start.4 = (f32[4,2,128,128]{3,2,1,0:T(8,128)S(1)}, f32[4,2,128,128]{3,2,1,0:T(8,128)}, u32[]{:S(2)}) copy-start(f32[4,2,128,128]{3,2,1,0:T(8,128)} %fusion.28) | copy-start | bytes 1572868
  148.8 3.6 copy-start.2
  414.8 56.9 %copy-start.1 = (f32[32,512]{1,0:T(8,128)S(1)}, f32[32,512]{1,0:T(8,128)}, u32[]{:S(2)}) copy-start(f32[32,512]{1,0:T(8,128)} %param.17) | copy-start | bytes 196612
Sparse Core Ops, SparseCore 0:
  44.4 83.4 all-gather.7
  129.4 285.2 all-gather.5
  428.9 42.6 reduce-scatter.1
where the time goes:
time: 479 us; the launch traced here: 478 us
  waiting for transfers between devices  366 us (76%)
  matrix products  32.8 us (7%)
  other arithmetic  28.8 us (6%)
  local copies, waits for them, and re-layouts  23.7 us (5%)
  between operations  13.3 us (3%)
  blocking collectives  12.9 us (3%)
    all_gather x1, waiting for transfers between devices, shards(): lax.all_gather(out_weight, 'ctx', axis=1, tiled=True)  259 us
    all_gather x1, waiting for transfers between devices, carried_in(): lax.all_gather(part.astype(kind), axis)  63.6 us
    reduce_scatter x1, waiting for transfers between devices, shards(): lax.psum_scatter(terms.astype(jnp.bfloat16), 'head', scatter_dimension=0,...  42.8 us
    dot_general x1, matrix products, shards(): jnp.dot(normed, lax.all_gather(out_weight, 'ctx', axis=1, tiled=True), pr...  14 us
    reshape x2, local copies, waits for them, and re-layouts, shards(): inputs = head_input.reshape(blocks, STRETCH, groups, per_group, HEADP)  13.6 us
    all_gather x1, blocking collectives, carried_in(): lax.all_gather(part.astype(kind), axis)  12.9 us
  transfers between devices with their start and end apart: 3, of which 3 were waited for; matrix products, arithmetic and copies ran while one was open for 7% of the time, Pallas kernels for 0%

commit v1 on v0

--- a/solution.py
+++ b/solution.py
@@ -6,6 +6,24 @@
 HEADP = 64
 STATE = 256
 STRETCH = 128
+
+
+def ring_gather(shard, axis, dim):
+    ways, here, step = (lax.axis_size(axis), lax.axis_index(axis), shard.shape[dim])
+    lengths = [n * ways if d == dim else n for d, n in enumerate(shard.shape)]
+    full = lax.dynamic_update_slice_in_dim(
+        jnp.zeros(lengths, shard.dtype), shard, here * step, axis=dim
+    )
+    going_up = going_down = shard
+    for far in range(1, ways // 2 + 1):
+        going_up = lax.ppermute(going_up, axis, [(d, (d + 1) % ways) for d in range(ways)])
+        full = lax.dynamic_update_slice_in_dim(full, going_up, (here - far) % ways * step, axis=dim)
+        if 2 * far < ways:
+            going_down = lax.ppermute(going_down, axis, [(d, (d - 1) % ways) for d in range(ways)])
+            full = lax.dynamic_update_slice_in_dim(
+                full, going_down, (here + far) % ways * step, axis=dim
+            )
+    return full
 
 
 def carried_in(shard, axis, combine, identity):
@@ -119,11 +137,7 @@
     normed = ((grouped * factor).reshape(tok_rows, width) * norm_gain.astype(jnp.float32)).astype(
         jnp.bfloat16
     )
-    terms = jnp.dot(
-        normed,
-        lax.all_gather(out_weight, "ctx", axis=1, tiled=True),
-        preferred_element_type=jnp.float32,
-    )
+    terms = jnp.dot(normed, ring_gather(out_weight, "ctx", 1), preferred_element_type=jnp.float32)
     summed = lax.psum_scatter(terms.astype(jnp.bfloat16), "head", scatter_dimension=0, tiled=True)
     return summed
 

time: 479 us -> 472 us (0.985)
  waiting for transfers between devices: 366 us -> 99.3 us
  blocking collectives: 12.9 us -> 246 us
  local copies, waits for them, and re-layouts: 23.7 us -> 45.9 us
  starting transfers between devices: 0.08 us -> 5.35 us
    all_gather x1 -> x0, waiting for transfers between devices: 259 us -> none  [shards(): lax.all_gather(out_weight, 'ctx', axis=1, tiled=True)]
    all_gather x1, blocking collectives: 12.9 us -> 246 us  [carried_in(): lax.all_gather(part.astype(kind), axis)]
    all_gather x1, waiting for transfers between devices: 63.6 us -> 0.01 us  [carried_in(): lax.all_gather(part.astype(kind), axis)]
    ppermute x0 -> x3, waiting for transfers between devices: none -> 56.4 us  [the longest x2 56.4 us: ring_gather(): lax.ppermute(going_up, axis, [(d, (d + 1) % ways) for d in range(ways)])]
    dynamic_update_slice x0 -> x4, local copies, waits for them, and re-layouts: none -> 16.3 us  [the longest x2 9.26 us: ring_gather(): lax.dynamic_update_slice_in_dim(full, going_up, (here - far) % ways * ste...]
    broadcast_in_dim x0 -> x1, local copies, waits for them, and re-layouts: none -> 6.65 us  [ring_gather(): jnp.zeros(lengths, shard.dtype)]
    ppermute x0 -> x3, starting transfers between devices: none -> 5.31 us  [the longest x2 3.22 us: ring_gather(): lax.ppermute(going_up, axis, [(d, (d + 1) % ways) for d in range(ways)])]
  transfers between devices with their start and end apart: 3 -> 5, of which waited for: 3 -> 2; matrix products, arithmetic and copies ran while one was open for 7% -> 11% of each run, Pallas kernels for 0% -> 0%
where the time goes in v1:
time: 472 us; the launch traced here: 471 us
  blocking collectives  246 us (52%)
  waiting for transfers between devices  99.3 us (21%)
  local copies, waits for them, and re-layouts  45.9 us (10%)
  matrix products  32 us (7%)
  other arithmetic  28.8 us (6%)
  between operations  13.6 us (3%)
  starting transfers between devices  5.35 us (1%)
    all_gather x1, blocking collectives, carried_in(): lax.all_gather(part.astype(kind), axis)  246 us
    ppermute x2, waiting for transfers between devices, ring_gather(): lax.ppermute(going_up, axis, [(d, (d + 1) % ways) for d in range(ways)])  56.4 us
    reduce_scatter x1, waiting for transfers between devices, shards(): lax.psum_scatter(terms.astype(jnp.bfloat16), 'head', scatter_dimension=0,...  42.9 us
    dot_general x1, matrix products, shards(): jnp.dot(normed, ring_gather(out_weight, 'ctx', 1), preferred_element_type...  14 us
    reshape x2, local copies, waits for them, and re-layouts, shards(): inputs = head_input.reshape(blocks, STRETCH, groups, per_group, HEADP)  13.7 us
  transfers between devices with their start and end apart: 5, of which 2 were waited for; matrix products, arithmetic and copies ran while one was open for 11% of the time, Pallas kernels for 0%

profile of v1, /device:TPU:0, one launch (start us, length us, event | category | flops | bytes accessed | tf_op | source)
XLA Modules:
  0.0 471.3 jit_solution(1724016057343705613)
XLA Ops:
  6.5 7.1 %reshape.83 = bf16[4,128,2,16,64]{4,3,2,1,0:T(8,128)(2,1)} reshape(bf16[512,2048]{1,0:T(8,128)(2,1)} %param.13) | data formatting | bytes 4194304 | tf_op jit(solution)/shard_map/reshape | solution.py:100
  13.6 6.6 %copy.27 = bf16[4,128,2,16,64]{1,4,3,2,0:T(8,128)(2,1)} copy(bf16[4,128,2,16,64]{4,3,2,1,0:T(8,128)(2,1)} %reshape.83) | data formatting | bytes 4194304 | tf_op jit(solution)/shard_map/reshape | solution.py:100
  21.9 6.1 %fusion.23 = f32[4,2,16,64,256]{4,3,2,1,0:T(8,128)} fusion(bf16[4,128,2,16,64]{1,4,3,2,0:T(8,128)(2,1)} %copy.27, f32[4,128,2,16]{1,3,2,0:T(8,128)S(1)} %bitcast.92, bf16[4,128,2,256,1]{3,2,1,0,4:T(2,128)(2,1)S(1)} %bitcast.89), kind=kOutput, calls=%fused_computation.39 | convolution fusion | flops 540016640 | bytes 11075584 | tf_op jit(solution)/shard_map/ksgjp,ksgn->kgjpn/dot_general | solution.py:68
  28.0 14.5 %while.31 = (s32[]{:T(128)}, f32[2,16,64,256]{3,2,1,0:T(8,128)S(1)}, f32[2,16]{1,0:T(2,128)S(1)}, f32[4,2,16,64,256]{4,3,2,1,0:T(8,128)}, f32[4,2,16]{2,1,0:T(2,...) while((s32[]{:T(128)}, ...), condition=%wide.region_2.3_spmd.clone, body=%wide.region_1.2_spmd.clone.sunk | while | flops 2097251 | bytes 10488578 | solution.py:116
  43.7 3.1 collective-permute-start
  46.8 2.1 collective-permute-start.1
  48.9 3.9 copy.32
  54.1 246.2 %all-gather.2 = bf16[4,2,16]{2,1,0:T(2,128)(2,1)S(1)} all-gather(bf16[1,2,16]{2,1,0:T(2,128)(2,1)S(1)} %convert_bitcast_fusion), channel_id=2, replica_groups=mesh['group'=2,'ctx'=4,'head'=4] {'ctx'}, dimensions={0}, use_global_device_ids=true | all-gather | bytes 320 | tf_op jit(solution)/shard_map/all_gather | solution.py:32
  301.4 6.6 %broadcast_in_dim.54 = bf16[2048,4096]{1,0:T(8,128)(2,1)} broadcast(bf16[]{:T(256)} %constant.84.clone.1), dimensions={} | broadcast | bytes 16777218 | tf_op jit(solution)/shard_map/broadcast_in_dim | solution.py:15
  308.1 2.5 constant_dynamic-update-slice_fusion.3
  310.7 4.7 constant_dynamic-update-slice_fusion.2
  315.4 4.6 constant_dynamic-update-slice_fusion.1
  320.0 9.0 %while.32 = (s32[]{:T(128)}, f32[2,16,64,256]{3,2,1,0:T(8,128)S(1)}, s32[]{:T(128)}, bf16[4,2,16]{2,1,0:T(2,128)(2,1)S(1)}, bf16[4,2,16,64,256]{4,3,2,1,0:T(8,128)(2,1)}, /*index=5*/s32[]{:T(128)}, s32[]{:T(128)}) while((s32[]{:T(128)}, f32[2,16,64,256]{3,2,1,0:T(8,128)S(1)}, s32[]{:T(128)}, bf16[4,2,16]{2,1,0:T(2,128)(2,1)S(1)}, ...), condition=%wide.region_4.5_spmd.clone, body=%wide.region_3.4_spmd.clone.sunk | while | flops 2621476 | bytes 5243313 | solution.py:49
  320.0 2.2 fusion.40
  322.2 2.2 fusion.40
  324.5 2.2 fusion.40
  326.8 2.2 fusion.40
  329.0 7.2 %fusion.2 = f32[4,2,16,64,128]{4,3,2,1,0:T(8,128)S(1)} fusion(f32[4,2,16,64,256]{4,3,2,1,0:T(8,128)} %get-tuple-element.139, f32[2,16,64,256]{3,2,1,0:T(8,128)S(1)} %get-tuple-element.143, f32[4,2,16]{2,1,0:T(2,128)S(1)} %get-tuple-element.140, bf16[4,128,2,256,1]{3,2,1,0,4:T(2,128)(2,1)S(1)} %bitcast.88), kind=kOutput, calls=%fused_computation.9 | convolution fusion | flops 3225419776 | bytes 15204864 | tf_op jit(solution)/shard_map/kqgn,kgjpn->kqgjp/dot_general | solution.py:124
  336.2 3.6 fusion.7
  339.9 3.6 copy.31
  346.6 56.4 %collective-permute-done.2 = bf16[2048,1024]{1,0:T(8,128)(2,1)} collective-permute-done((bf16[2048,1024]{1,0:T(8,128)(2,1)}, bf16[2048,1024]{1,0:T(8,128)(2,1)}, u32[]{:S(2)}, u32[]{:S(2)}) %collective-permute-start.2) | collective-permute-done | bytes 4194336 | tf_op jit(solution)/shard_map/ppermute | solution.py:19
  403.0 4.6 constant_dynamic-update-slice_fusion
  407.6 14.0 %convolution_convert_fusion = bf16[512,4096]{1,0:T(8,128)(2,1)} fusion(bf16[512,2048]{0,1:T(8,128)(2,1)S(1)} %fusion.13, bf16[2048,4096]{1,0:T(8,128)(2,1)} %constant_dynamic-update-slice_fusion), kind=kOutput, calls=%fused_computation.13 | convolution fusion | flops 8592031744 | bytes 23068672 | tf_op jit(solution)/shard_map/dot_general | solution.py:140
  421.6 42.9 %reduce-scatter.2.cloned.1.call-done = bf16[128,4096]{1,0:T(8,128)(2,1)} async-done(((bf16[512,4096]{1,0:T(8,128)(2,1)}), bf16[128,4096]{1,0:T(8,128)(2,1)}) %reduce-scatter.2.cloned.1.call-update) | async-done | bytes 1048592 | tf_op jit(solution)/shard_map/reduce_scatter | solution.py:141
  (71 shorter events, 23.0 us)
Async XLA Ops:
  6.5 15.3 %copy-start = (f32[32,512]{1,0:T(8,128)S(1)}, f32[32,512]{1,0:T(8,128)}, u32[]{:S(2)}) copy-start(f32[32,512]{1,0:T(8,128)} %param.17) | copy-start | bytes 196612
  6.5 313.4 %all-gather.5.cloned.1.call-start = ((), (), s32[]{:S(2)}) async-start(), calls=%async_computation.2 | async-start | bytes 5242880 | tf_op jit(solution)/shard_map/all_gather | solution.py:32
  13.6 6.6 %copy-start.7 = (f32[32,512]{1,0:T(8,128)S(1)}, f32[32,512]{1,0:T(8,128)}, u32[]{:S(2)}) copy-start(f32[32,512]{1,0:T(8,128)} %param.18) | copy-start | bytes 196612
  13.6 8.0 %copy-start.6 = (bf16[512,512]{1,0:T(8,128)(2,1)S(1)}, bf16[512,512]{1,0:T(8,128)(2,1)}, u32[]{:S(2)}) copy-start(bf16[512,512]{1,0:T(8,128)(2,1)} %param.15) | copy-start | bytes 1572868
  42.5 6.4 %copy-start.8 = (bf16[2048]{0:T(1024)(128)(2,1)S(1)}, bf16[2048]{0:T(1024)(128)(2,1)}, u32[]{:S(2)}) copy-start(bf16[2048]{0:T(1024)(128)(2,1)} %param.20) | copy-start | bytes 12292
  42.5 11.5 %copy-start.9 = (f32[32]{0:T(128)S(1)}, f32[32]{0:T(128)}, u32[]{:S(2)}) copy-start(f32[32]{0:T(128)} %param.19) | copy-start | bytes 388
  43.7 420.8 %reduce-scatter.2.cloned.1.call-start = ((), (), s32[]{:S(2)}) async-start(), calls=%async_computation.1 | async-start | bytes 5242880 | tf_op jit(solution)/shard_map/reduce_scatter | solution.py:141
  43.7 266.8 %collective-permute-start = (bf16[2048,1024]{1,0:T(8,128)(2,1)}, bf16[2048,1024]{1,0:T(8,128)(2,1)}, u32[]{:S(2)}, u32[]{:S(2)}) collective-permute-start(bf16[2048,1024]{1,0:T(8,128)(2,1)} %param.21), channel_id=1, source_target_pairs={{0,4},{4,8},{8,12},{12,0},{1,5},{5,9},{9,13},{13,1},{2,6},{6,10},{... | collective-permute-start | bytes 12582920 | tf_op jit(solution)/shard_map/ppermute | solution.py:19
  46.8 268.6 %collective-permute-start.1 = (bf16[2048,1024]{1,0:T(8,128)(2,1)}, bf16[2048,1024]{1,0:T(8,128)(2,1)}, u32[]{:S(2)}, u32[]{:S(2)}) collective-permute-start(bf16[2048,1024]{1,0:T(8,128)(2,1)} %param.21), channel_id=1, source_target_pairs={{0,12},{4,0},{8,4},{12,8},{1,13},{5,1},{9,5},{13,9},{2,14},{6,2},{... | collective-permute-start | bytes 12582920 | tf_op jit(solution)/shard_map/ppermute | solution.py:22
  301.4 6.7 %copy-start.4 = (bf16[2048,1024]{1,0:T(8,128)(2,1)S(1)}, bf16[2048,1024]{1,0:T(8,128)(2,1)}, u32[]{:S(2)}) copy-start(bf16[2048,1024]{1,0:T(8,128)(2,1)} %param.21) | copy-start | bytes 12582916
  310.6 92.4 %collective-permute-start.2 = (bf16[2048,1024]{1,0:T(8,128)(2,1)}, bf16[2048,1024]{1,0:T(8,128)(2,1)}, u32[]{:S(2)}, u32[]{:S(2)}) collective-permute-start(bf16[2048,1024]{1,0:T(8,128)(2,1)} %collective-permute-done), channel_id=1, source_target_pairs={{0,4},{4,8},{8,12},{12,0},{1,5},{5,9},{9,13},{13,1},{2,6},{6,10},{... | collective-permute-start | bytes 12582920 | tf_op jit(solution)/shard_map/ppermute | solution.py:19
  329.0 7.2 %copy-start.3 = (bf16[4,128,2,16,64]{1,4,3,2,0:T(8,128)(2,1)S(1)}, bf16[4,128,2,16,64]{1,4,3,2,0:T(8,128)(2,1)}, u32[]{:S(2)}) copy-start(bf16[4,128,2,16,64]{1,4,3,2,0:T(8,128)(2,1)} %copy.27) | copy-start | bytes 6291460
  329.0 7.2 %copy-start.5 = (f32[4,2,128,128]{3,2,1,0:T(8,128)S(1)}, f32[4,2,128,128]{3,2,1,0:T(8,128)}, u32[]{:S(2)}) copy-start(f32[4,2,128,128]{3,2,1,0:T(8,128)} %fusion.28) | copy-start | bytes 1572868
  339.9 3.6 copy-start.2
  407.6 56.9 %copy-start.1 = (f32[32,512]{1,0:T(8,128)S(1)}, f32[32,512]{1,0:T(8,128)}, u32[]{:S(2)}) copy-start(f32[32,512]{1,0:T(8,128)} %param.17) | copy-start | bytes 196612
Sparse Core Ops, SparseCore 0:
  43.8 197.4 all-gather.4
  421.7 42.7 reduce-scatter.1
